TPU v7x, 32 devices: a whole 2x2x4 slice. The times are simulated.
32 devices in a mesh: row: 8 (over z, x), col: 4 (over y, core).
Axes of the slice: x: 2, y: 2, z: 4, core: 2. Of those that a mesh axis runs over, the one named last changes fastest.
Arguments:
- vertex: bfloat16 [64, 4096, 4096], P(None, 'row', 'col'), may hold values from -6 to 6
- a_factor: bfloat16 [4096, 1024], P('row', 'col'), as said below
- b_factor: bfloat16 [4096, 1024], P('col', 'row'), as said below
Outputs:
- field_factor: float32 [64, 1024], P(None, 'col')
Inputs may be any that keep to these rules, and one draw needn't show every extreme that they name: `a_factor`: entries lie within -12 / sqrt(4096) and 12 / sqrt(4096). `b_factor`: entries lie within -12 / sqrt(4096) and 12 / sqrt(4096).
All inputs are finite; a program needn't handle non-finite values.
Results may differ from a plain program's by a relative error of at most 0.0003.
Values may be sent and summed in bfloat16 or wider, within the bound.
No kernel may reach another device: no remote copies, remote signals or barrier semaphores. Data moves between devices by JAX's collectives and lax.ppermute only.
A program may use at most 128 MiB of HBM per device.

v0:
```python
import jax
import jax.numpy as jnp
from jax import lax
from jax.sharding import PartitionSpec as P

ridge_term = 0.25


def on_device(vertex, a_factor, b_factor):
    fields, p_local, q_local = vertex.shape
    rank_cols = a_factor.shape[1]
    row_rank = b_factor.shape[1]
    a_rows = lax.all_gather(a_factor, "col", axis=1, tiled=True)
    total_rank = a_rows.shape[1]
    groups = fields // 4
    stacked = vertex.reshape(groups, 4 * p_local, q_local)
    column_block = lax.all_gather(b_factor, "row", axis=1, tiled=True)
    width_now = column_block.shape[1]
    a_cols = a_rows.astype(jnp.float32)

    def one_group(slab):
        product = jnp.dot(slab, column_block, preferred_element_type=jnp.float32)
        product = product.reshape(4, p_local, width_now) * a_cols[None]
        return jnp.sum(product, axis=1)

    field_part = lax.map(one_group, stacked).reshape(fields, width_now)
    gram_part = lax.dot_general(
        b_factor, column_block, (((0,), (0,)), ((), ())), preferred_element_type=jnp.float32
    )
    joined = jnp.concatenate([field_part, gram_part], axis=0)
    m_part = joined[:fields]
    gb_part = joined[fields:]
    ga_part = lax.dot_general(
        a_factor, a_rows, (((0,), (0,)), ((), ())), preferred_element_type=jnp.float32
    )
    m_total = lax.psum(m_part, ("row", "col"))
    ga_tile = lax.psum_scatter(ga_part, "row", scatter_dimension=1, tiled=True)
    gb_tile = lax.psum_scatter(gb_part, "col", scatter_dimension=1, tiled=True)
    product_tile = ga_tile * gb_tile.T
    tiles = lax.all_gather(product_tile[None], ("row", "col"), axis=0, tiled=True)
    row_count = lax.axis_size("row")
    col_count = lax.axis_size("col")
    weight = (
        tiles.reshape(row_count, col_count, rank_cols, row_rank)
        .transpose(1, 2, 0, 3)
        .reshape(total_rank, total_rank)
    )
    weight = weight + ridge_term * jnp.eye(total_rank, dtype=jnp.float32)
    factor_lower = jnp.linalg.cholesky(weight)
    solved = jax.scipy.linalg.cho_solve((factor_lower, True), m_total.T)
    col_index = lax.axis_index("col")
    return lax.dynamic_slice_in_dim(solved.T, col_index * rank_cols, rank_cols, 1)


def solution(mesh):
    return jax.shard_map(
        on_device,
        mesh=mesh,
        in_specs=(P(None, "row", "col"), P("row", "col"), P("col", "row")),
        out_specs=P(None, "col"),
        check_vma=False,
    )
```

profile of v0, /device:TPU:0, one launch (start us, length us, event | category | flops | bytes accessed | tf_op | source)
XLA Modules:
  0.0 671.2 jit_solution(9382028890872371031)
XLA Ops:
  8.1 20.4 %all-gather.5.cloned.1.call-done = bf16[512,1024]{1,0:T(8,128)(2,1)} async-done(((bf16[512,256]{1,0:T(8,128)(2,1)}), bf16[512,1024]{1,0:T(8,128)(2,1)}) %all-gather.5.cloned.1.call-update) | async-done | bytes 1048592 | tf_op jit(solution)/shard_map/all_gather | solution.py:13
  28.5 2.9 fusion.96
  31.5 50.2 %all-gather.7.cloned.1.call-done = bf16[1024,1024]{1,0:T(8,128)(2,1)} async-done(((bf16[1024,128]{1,0:T(8,128)(2,1)}), bf16[1024,1024]{1,0:T(8,128)(2,1)}) %all-gather.7.cloned.1.call-update) | async-done | bytes 2097168 | tf_op jit(solution)/shard_map/all_gather | solution.py:17
  81.6 3.4 fusion.97
  85.4 61.8 %reduce-scatter.3.cloned.1.call-done = f32[256,128]{1,0:T(8,128)} async-done(((f32[256,1024]{1,0:T(8,128)}), f32[256,128]{1,0:T(8,128)}) %reduce-scatter.3.cloned.1.call-update) | async-done | bytes 131088 | tf_op jit(solution)/shard_map/reduce_scatter | solution.py:37
  147.2 23.2 %reduce-scatter.5.cloned.1.call-done = f32[128,256]{0,1:T(8,128)} async-done(((f32[128,1024]{0,1:T(8,128)}), f32[128,256]{0,1:T(8,128)}) %reduce-scatter.5.cloned.1.call-update) | async-done | bytes 131088 | tf_op jit(solution)/shard_map/reduce_scatter | solution.py:38
  172.1 123.0 %while.11 = (s32[]{:T(128)}, f32[16,4,1024]{2,1,0:T(4,128)S(1)}, bf16[16,2048,1024]{2,1,0:T(8,128)(2,1)}, bf16[1024,1024]{1,0:T(8,128)(2,1)}, f32[512,1024]{1,0:T(8,128)S(1)}, /*index=5*/s32[]{:T(128)}) while((s32[]{:T(128)}, f32[16,4,1024]{2,1,0:T(4,128)S(1)}, bf16[16,2048,1024]{2,1,0:T(8,128)(2,1)}, bf16[1024,1024]{1,0:T(8,128)(2,1)}, ...), condition=%wide.region_20.21_spmd, body=%wide.region_18.20_spmd.sunk | while | flops 4299157504 | bytes 25215088 | solution.py:26
  172.1 2.8 constant_dynamic-slice_fusion.4
  175.0 4.8 multiply_reduce_fusion.2
  179.8 2.9 constant_dynamic-slice_fusion.4
  182.8 4.8 multiply_reduce_fusion.2
  190.4 4.8 multiply_reduce_fusion.2
  195.3 2.8 constant_dynamic-slice_fusion.4
  198.1 4.8 multiply_reduce_fusion.2
  202.9 2.8 constant_dynamic-slice_fusion.4
  205.8 4.8 multiply_reduce_fusion.2
  210.6 2.8 constant_dynamic-slice_fusion.4
  213.5 4.8 multiply_reduce_fusion.2
  218.3 2.8 constant_dynamic-slice_fusion.4
  221.1 4.8 multiply_reduce_fusion.2
  226.0 2.9 constant_dynamic-slice_fusion.4
  228.9 4.8 multiply_reduce_fusion.2
  233.7 2.8 constant_dynamic-slice_fusion.4
  236.6 4.8 multiply_reduce_fusion.2
  241.5 2.8 constant_dynamic-slice_fusion.4
  244.3 4.8 multiply_reduce_fusion.2
  249.1 2.8 constant_dynamic-slice_fusion.4
  252.0 4.8 multiply_reduce_fusion.2
  256.8 2.8 constant_dynamic-slice_fusion.4
  259.6 4.8 multiply_reduce_fusion.2
  264.5 2.8 constant_dynamic-slice_fusion.4
  267.3 4.8 multiply_reduce_fusion.2
  272.1 2.8 constant_dynamic-slice_fusion.4
  275.0 4.8 multiply_reduce_fusion.2
  279.8 2.8 constant_dynamic-slice_fusion.4
  282.7 4.8 multiply_reduce_fusion.2
  287.5 2.8 constant_dynamic-slice_fusion.4
  290.3 4.8 multiply_reduce_fusion.2
  296.0 5.2 copy.5
  301.2 3.2 copy.31
  308.7 5.5 copy.6
  314.3 4.5 fusion.1
  320.7 11.7 %cholesky.222 = f32[128,128]{1,0:T(8,128)S(1)} custom-call(f32[128,128]{1,0:T(8,128)S(1)} %cholesky.577), custom_call_target="Cholesky" | custom-call | tf_op jit(solution)/shard_map/jit(cholesky)/cholesky | solution.py:49
  332.5 9.8 %custom-call.66 = f32[1,128,128]{1,2,0:T(8,128)S(1)} custom-call(f32[1,128,128]{2,1,0:T(8,128)S(1)} %get-tuple-element.78), custom_call_target="InvertDiagBlocksLowerTriangular" | custom-call | tf_op jit(solution)/shard_map/jit(cholesky)/cholesky | solution.py:49
  345.7 11.7 %cholesky.243 = f32[128,128]{1,0:T(8,128)S(1)} custom-call(f32[128,128]{1,0:T(8,128)S(1)} %cholesky.581), custom_call_target="Cholesky" | custom-call | tf_op jit(solution)/shard_map/jit(cholesky)/cholesky | solution.py:49
  357.7 9.8 %custom-call.67 = f32[1,128,128]{1,2,0:T(8,128)S(1)} custom-call(f32[1,128,128]{2,1,0:T(8,128)S(1)} %get-tuple-element.76), custom_call_target="InvertDiagBlocksLowerTriangular" | custom-call | tf_op jit(solution)/shard_map/jit(cholesky)/cholesky | solution.py:49
  373.1 11.7 %cholesky.466 = f32[128,128]{1,0:T(8,128)S(1)} custom-call(f32[128,128]{1,0:T(8,128)S(1)} %cholesky.586), custom_call_target="Cholesky" | custom-call | tf_op jit(solution)/shard_map/jit(cholesky)/cholesky | solution.py:49
  385.5 9.8 %custom-call.68 = f32[1,128,128]{1,2,0:T(8,128)S(1)} custom-call(f32[1,128,128]{2,1,0:T(8,128)S(1)} %get-tuple-element.74), custom_call_target="InvertDiagBlocksLowerTriangular" | custom-call | tf_op jit(solution)/shard_map/jit(cholesky)/cholesky | solution.py:49
  396.6 3.5 convolution_subtract_fusion.2
  400.2 11.7 %cholesky.485 = f32[128,128]{1,0:T(8,128)S(1)} custom-call(f32[128,128]{1,0:T(8,128)S(1)} %cholesky.591), custom_call_target="Cholesky" | custom-call | tf_op jit(solution)/shard_map/jit(cholesky)/cholesky | solution.py:49
  412.7 9.8 %custom-call.69 = f32[1,128,128]{1,2,0:T(8,128)S(1)} custom-call(f32[1,128,128]{2,1,0:T(8,128)S(1)} %get-tuple-element.72), custom_call_target="InvertDiagBlocksLowerTriangular" | custom-call | tf_op jit(solution)/shard_map/jit(cholesky)/cholesky | solution.py:49
  423.6 3.1 convolution_subtract_fusion.3
  426.8 11.9 %cholesky.504 = f32[128,128]{1,0:T(8,128)S(1)} custom-call(f32[128,128]{1,0:T(8,128)S(1)} %cholesky.596), custom_call_target="Cholesky" | custom-call | tf_op jit(solution)/shard_map/jit(cholesky)/cholesky | solution.py:49
  439.4 9.8 %custom-call.70 = f32[1,128,128]{1,2,0:T(8,128)S(1)} custom-call(f32[1,128,128]{2,1,0:T(8,128)S(1)} %get-tuple-element.70), custom_call_target="InvertDiagBlocksLowerTriangular" | custom-call | tf_op jit(solution)/shard_map/jit(cholesky)/cholesky | solution.py:49
  450.4 3.1 convolution_subtract_fusion.4
  453.4 11.7 %cholesky.524 = f32[128,128]{1,0:T(8,128)S(1)} custom-call(f32[128,128]{1,0:T(8,128)S(1)} %cholesky.601), custom_call_target="Cholesky" | custom-call | tf_op jit(solution)/shard_map/jit(cholesky)/cholesky | solution.py:49
  465.9 9.8 %custom-call.71 = f32[1,128,128]{1,2,0:T(8,128)S(1)} custom-call(f32[1,128,128]{2,1,0:T(8,128)S(1)} %get-tuple-element.68), custom_call_target="InvertDiagBlocksLowerTriangular" | custom-call | tf_op jit(solution)/shard_map/jit(cholesky)/cholesky | solution.py:49
  476.7 2.9 convolution_subtract_fusion.5
  479.6 11.7 %cholesky.544 = f32[128,128]{1,0:T(8,128)S(1)} custom-call(f32[128,128]{1,0:T(8,128)S(1)} %cholesky.606), custom_call_target="Cholesky" | custom-call | tf_op jit(solution)/shard_map/jit(cholesky)/cholesky | solution.py:49
  492.1 9.8 %custom-call.72 = f32[1,128,128]{1,2,0:T(8,128)S(1)} custom-call(f32[1,128,128]{2,1,0:T(8,128)S(1)} %get-tuple-element.66), custom_call_target="InvertDiagBlocksLowerTriangular" | custom-call | tf_op jit(solution)/shard_map/jit(cholesky)/cholesky | solution.py:49
  504.9 11.7 %cholesky.562 = f32[128,128]{1,0:T(8,128)S(1)} custom-call(f32[128,128]{1,0:T(8,128)S(1)} %convolution_subtract_fusion.6), custom_call_target="Cholesky" | custom-call | tf_op jit(solution)/shard_map/jit(cholesky)/cholesky | solution.py:49
  527.0 4.8 select_select_fusion
  531.9 28.6 %while.12 = (s32[]{:T(128)}, f32[1024,1024]{0,1:T(8,128)}, s32[8,2]{0,1:T(2,128)S(1)}, f32[8,128,128]{2,1,0:T(8,128)}, s32[]{:T(128)}) while((s32[]{:T(128)}, f32[1024,1024]{0,1:T(8,128)}, s32[8,2]{0,1:T(2,128)S(1)}, f32[8,128,128]{2,1,0:T(8,128)}, s32[]{:T(128)}) %tuple.65), condition=%wide.while_cond, body=%wide.while_body.sunk | while | flops 2 | bytes 393329 | solution.py:50
  560.5 79.6 %custom-call.73 = f32[8,128,128]{1,2,0:T(8,128)S(1)} custom-call(f32[8,128,128]{2,1,0:T(8,128)} %get-tuple-element.40), custom_call_target="InvertDiagBlocksLowerTriangular" | custom-call | tf_op jit(solution)/shard_map/jit(_cho_solve)/triangular_solve | solution.py:50
  (222 shorter events, 92.5 us)
Async XLA Ops:
  6.5 22.0 %all-gather.5.cloned.1.call-start = ((), (), s32[]{:S(2)}) async-start(), calls=%async_computation.2 | async-start | bytes 1310720 | tf_op jit(solution)/shard_map/all_gather | solution.py:13
  7.3 74.4 %all-gather.7.cloned.1.call-start = ((), (), s32[]{:S(2)}) async-start(), calls=%async_computation.4 | async-start | bytes 2359296 | tf_op jit(solution)/shard_map/all_gather | solution.py:17
  8.0 139.2 %reduce-scatter.3.cloned.1.call-start = ((), (), s32[]{:S(2)}) async-start(), calls=%async_computation.3 | async-start | bytes 1179648 | tf_op jit(solution)/shard_map/reduce_scatter | solution.py:37
  28.5 56.7 %copy-start.3 = (bf16[512,1024]{1,0:T(8,128)(2,1)S(1)}, bf16[512,1024]{1,0:T(8,128)(2,1)}, u32[]{:S(2)}) copy-start(bf16[512,1024]{1,0:T(8,128)(2,1)} %all-gather.5.cloned.1.call-done) | copy-start | bytes 3145732
  31.4 139.0 %reduce-scatter.5.cloned.1.call-start = ((), (), s32[]{:S(2)}) async-start(), calls=%async_computation.5 | async-start | bytes 655360 | tf_op jit(solution)/shard_map/reduce_scatter | solution.py:38
  85.1 210.9 %all-gather.9.cloned.1.call-start = ((), (), s32[]{:S(2)}) async-start(), calls=%async_computation.7 | async-start | bytes 4325376 | tf_op jit(solution)/shard_map/all_gather | solution.py:40
  172.0 468.1 %all-reduce.3.cloned.1.call-start = ((), (), s32[]{:S(2)}) async-start(), calls=%async_computation.6 | async-start | bytes 524288 | tf_op jit(solution)/shard_map/psum | solution.py:36
  172.1 2.9 copy-start.4
  179.8 3.0 copy-start.4
  187.6 2.9 copy-start.4
  195.2 2.9 copy-start.4
  202.9 2.9 copy-start.4
  210.6 2.9 copy-start.4
  218.3 2.9 copy-start.4
  226.0 2.9 copy-start.4
  233.7 2.9 copy-start.4
  241.4 2.9 copy-start.4
  249.1 2.9 copy-start.4
  256.8 2.9 copy-start.4
  264.5 2.9 copy-start.4
  272.1 2.9 copy-start.4
  279.8 2.9 copy-start.4
  287.5 2.9 copy-start.4
  304.4 1.9 copy-start.1
  318.8 1.9 copy-start.2
  368.7 2.0 copy-start
Sparse Core Ops, SparseCore 0:
  8.9 19.5 all-gather.4
  30.5 51.0 all-gather.6
  85.0 62.1 reduce-scatter.2
  149.7 20.6 reduce-scatter.4
  173.1 62.0 all-gather.8
  296.1 125.8 all-reduce.2
where the time goes:
time: 678 us; the launch traced here: 671 us
  other arithmetic  261 us (38%)
  waiting for transfers between devices  157 us (23%)
  matrix products  132 us (19%)
  local copies, waits for them, and re-layouts  101 us (15%)
  between operations  19.6 us (3%)
    another operation x30, other arithmetic, on_device(): factor_lower = jnp.linalg.cholesky(weight)  167 us
    another operation x3, other arithmetic, on_device(): solved = jax.scipy.linalg.cho_solve((factor_lower, True), m_total.T)  84.5 us
    dot_general x16, matrix products, one_group(): product = jnp.dot(slab, column_block, preferred_element_type=jnp.float32)  76.5 us
    reduce_scatter x1, waiting for transfers between devices, on_device(): ga_tile = lax.psum_scatter(ga_part, 'row', scatter_dimension=1, tiled=True)  61.8 us
    all_gather x1, waiting for transfers between devices, on_device(): column_block = lax.all_gather(b_factor, 'row', axis=1, tiled=True)  50.2 us
    dynamic_slice x16, local copies, waits for them, and re-layouts, on_device(): field_part = lax.map(one_group, stacked).reshape(fields, width_now)  44.7 us
    another operation x40, local copies, waits for them, and re-layouts  28.5 us
    another operation x14, matrix products, on_device(): factor_lower = jnp.linalg.cholesky(weight)  26.2 us
  transfers between devices with their start and end apart: 6, of which 4 were waited for; matrix products, arithmetic and copies ran while one was open for 69% of the time, Pallas kernels for 0%

commit v1 on v0

v1 whole, which is shorter than its diff:
```python
import functools

import jax
import jax.numpy as jnp
from jax import lax
from jax.experimental import pallas as pl
from jax.experimental.pallas import tpu as pltpu
from jax.sharding import PartitionSpec as P

ridge_term = 0.25
NB = 128
HIGHEST = lax.Precision.HIGHEST
MIB = 1 << 20


def dot_nt(x, y):
    return lax.dot_general(
        x, y, (((1,), (1,)), ((), ())), precision=HIGHEST, preferred_element_type=jnp.float32
    )


def dot_nn(x, y):
    return lax.dot_general(
        x, y, (((1,), (0,)), ((), ())), precision=HIGHEST, preferred_element_type=jnp.float32
    )


def dot_tn(x, y):
    return lax.dot_general(x, y, (((0,), (0,)), ((), ())), preferred_element_type=jnp.float32)


def row_of(v, j):
    return jnp.broadcast_to(v[j : j + 1, :], v.shape)


def col_of(v, j):
    return jnp.broadcast_to(v[:, j : j + 1], v.shape)


def invert_factor(rows):
    count = len(rows)
    lane = lax.broadcasted_iota(jnp.int32, (8, NB), 1)
    sub = lax.broadcasted_iota(jnp.int32, (8, NB), 0)
    rows = list(rows)
    scale = [None] * count
    for g in range(count):
        base = 8 * g
        cur = rows[g]
        cols = [col_of(cur, base + j) for j in range(8)]
        below = [[col_of(rows[i], base + j) for j in range(8)] for i in range(g + 1, count)]
        own = (lane >= base) & (lane < base + 8)
        cur = jnp.where(own, jnp.where(lane == sub + base, 1.0, 0.0), cur)
        forward = cur
        inverse = None
        for j in range(8):
            inv = 1.0 / row_of(cols[j], j)
            here = sub == j
            pivot = row_of(cur, j)
            forward = jnp.where(here, cur, forward)
            inverse = inv if inverse is None else jnp.where(here, inv, inverse)
            mult = cols[j] * inv
            for k in range(j + 1, 8):
                ck = row_of(cols[k], j)
                cols[k] = jnp.where(here, ck * inv, cols[k] - mult * ck)
            cur = jnp.where(here, pivot * inv, cur - mult * pivot)
        picks = [row_of(cur, j) for j in range(8)]
        for t, i in enumerate(range(g + 1, count)):
            prods = [below[t][j] * picks[j] for j in range(8)]
            while len(prods) > 1:
                prods = [prods[s] + prods[s + 1] for s in range(0, len(prods), 2)]
            rows[i] = jnp.where(own, 0.0, rows[i]) - prods[0]
        rows[g] = forward
        scale[g] = jnp.sqrt(inverse)
    return [jnp.where(lane <= sub + 8 * g, rows[g], 0.0) * scale[g] for g in range(count)]


def blk(i):
    return pl.ds(pl.multiple_of(i * NB, NB), NB)


def factor_and_solve(work, z, linv):
    nk = work.shape[0]

    def step(k, _):
        rows = [work[k, pl.ds(pl.multiple_of(k * NB + 8 * g, 8), 8), :] for g in range(NB // 8)]
        for g, v in enumerate(invert_factor(rows)):
            linv[k, 8 * g : 8 * g + 8, :] = v
        inverse = linv[k]
        z[:, blk(k)] = dot_nt(z[:, blk(k)], inverse)

        def panel(i, _):
            work[k, blk(i), :] = dot_nt(work[k, blk(i), :], inverse)
            return 0

        lax.fori_loop(k + 1, nk, panel, 0)

        def column(j, _):
            pj = work[k, blk(j), :]
            z[:, blk(j)] -= dot_nt(z[:, blk(k)], pj)

            def tile(i, _):
                work[j, blk(i), :] -= dot_nt(work[k, blk(i), :], pj)
                return 0

            lax.fori_loop(j, nk, tile, 0)
            return 0

        lax.fori_loop(k + 1, nk, column, 0)
        return 0

    lax.fori_loop(0, nk, step, 0)

    def back(t, _):
        k = nk - 1 - t
        xk = dot_nn(z[:, blk(k)], linv[k])
        z[:, blk(k)] = xk

        def update(i, _):
            z[:, blk(i)] -= dot_nn(xk, work[i, blk(k), :])
            return 0

        lax.fori_loop(0, k, update, 0)
        return 0

    lax.fori_loop(0, nk, back, 0)


def solve_kernel(tiles, pos, *refs):
    pieces, (m_ref, x_ref, work, z, linv, sem) = refs[: len(tiles)], refs[len(tiles) :]
    copies = []
    for piece, offsets in zip(pieces, tiles):
        for t, (row_off, col_off) in enumerate(offsets):
            height = piece.shape[1]
            at = pl.multiple_of((pos[1] ^ col_off) * height, height)
            target = work.at[pos[0] ^ row_off, pl.ds(at, height), :]
            copies.append(pltpu.make_async_copy(piece.at[t], target, sem.at[len(copies)]))
            copies[-1].start()
    z[...] = m_ref[...]
    for copy in copies:
        copy.wait()
    factor_and_solve(work, z, linv)
    x_ref[...] = z[...]


def solve(pos, pieces, tiles, m_total):
    rank = m_total.shape[1]
    total = sum(len(t) for t in tiles)
    return pl.pallas_call(
        functools.partial(solve_kernel, tiles),
        out_shape=jax.ShapeDtypeStruct(m_total.shape, jnp.float32),
        in_specs=[pl.BlockSpec(memory_space=pltpu.SMEM)]
        + [pl.BlockSpec(memory_space=pl.ANY)] * len(pieces)
        + [pl.BlockSpec(memory_space=pltpu.VMEM)],
        out_specs=pl.BlockSpec(memory_space=pltpu.VMEM),
        scratch_shapes=[
            pltpu.VMEM((rank // NB, rank, NB), jnp.float32),
            pltpu.VMEM(m_total.shape, jnp.float32),
            pltpu.VMEM((rank // NB, NB, NB), jnp.float32),
            pltpu.SemaphoreType.DMA((total,)),
        ],
        compiler_params=pltpu.CompilerParams(vmem_limit_bytes=24 * MIB),
        cost_estimate=pl.CostEstimate(flops=40_000_000_000, bytes_accessed=4 * rank * rank, transcendentals=0),
    )(pos, *pieces, m_total)


def contract_kernel(index, v_ref, b_ref, a_ref, o_ref):
    fields, p_local, q_local = v_ref.shape
    for n in range(b_ref.shape[0]):
        width = b_ref.shape[2]
        at = pl.multiple_of(index[n] * width, width)
        a_cols = a_ref[:, pl.ds(at, width)]
        for f in range(fields):
            product = jnp.dot(v_ref[f], b_ref[n], preferred_element_type=jnp.float32)
            o_ref[0, f : f + 1, n * width : (n + 1) * width] = jnp.sum(product * a_cols, axis=0, keepdims=True)


def contract(index, vertex, b_blocks, a_wide):
    fields, p_local, q_local = vertex.shape
    count, _, width = b_blocks.shape
    step = 4
    out = pl.pallas_call(
        contract_kernel,
        out_shape=jax.ShapeDtypeStruct((fields // step, step, count * width), jnp.float32),
        grid_spec=pltpu.PrefetchScalarGridSpec(
            num_scalar_prefetch=1,
            grid=(fields // step,),
            in_specs=[
                pl.BlockSpec((step, p_local, q_local), lambda i, s: (i, 0, 0)),
                pl.BlockSpec(b_blocks.shape, lambda i, s: (0, 0, 0)),
                pl.BlockSpec(a_wide.shape, lambda i, s: (0, 0)),
            ],
            out_specs=pl.BlockSpec((1, step, count * width), lambda i, s: (i, 0, 0)),
        ),
        compiler_params=pltpu.CompilerParams(vmem_limit_bytes=40 * MIB),
        cost_estimate=pl.CostEstimate(
            flops=2 * fields * p_local * q_local * count * width,
            bytes_accessed=2 * fields * p_local * q_local,
            transcendentals=0,
        ),
    )(index, vertex, b_blocks, a_wide)
    return out.reshape(fields, count * width)


def swap(v, axis, bit):
    return lax.ppermute(v, axis, [(s, s ^ bit) for s in range(lax.axis_size(axis))])


def ordered(bit_set, mine, theirs, axis):
    return jnp.where(
        bit_set, jnp.concatenate([theirs, mine], axis), jnp.concatenate([mine, theirs], axis)
    )


def fast(vertex, a_factor, b_factor):
    row, col = lax.axis_index("row"), lax.axis_index("col")
    fields = vertex.shape[0]
    wide = a_factor.shape[1]
    narrow = b_factor.shape[1]
    rank = 4 * wide
    x_bit, z_low, z_high = row & 1, (row >> 1) & 1, row >> 2
    core, y_bit = col & 1, col >> 1
    zz = row >> 1

    b_pair = ordered(x_bit == 1, b_factor, swap(b_factor, "row", 1), 1)
    a_pair = ordered(y_bit == 1, a_factor, swap(a_factor, "col", 2), 1)
    b_far = swap(b_pair, "row", 4)
    a_other = swap(a_pair, "col", 1)
    own, other = a_pair.reshape(-1, 2, wide), a_other.reshape(-1, 2, wide)
    first = jnp.where(core == 1, other, own)
    second = jnp.where(core == 1, own, other)
    a_rows = jnp.stack([first, second], axis=2).reshape(-1, rank)
    a_wide = a_rows.astype(jnp.float32)
    b_half = jnp.stack([b_pair, b_far])
    b_rest = swap(b_half, "row", 2)

    ga = dot_tn(a_rows, a_factor).reshape(4, 2, narrow, wide)
    ga_send = jnp.where(x_bit == 1, ga[:, 0], ga[:, 1])
    ga_keep = jnp.where(x_bit == 1, ga[:, 1], ga[:, 0])
    ga = (ga_keep + swap(ga_send, "row", 1)).reshape(2, 2, narrow, wide)
    ga_send = jnp.where(z_low == 1, ga[:, 0], ga[:, 1])
    ga_keep = jnp.where(z_low == 1, ga[:, 1], ga[:, 0])
    ga = ga_keep + swap(ga_send, "row", 2)
    ga_send = jnp.where(z_high == 1, ga[0], ga[1])
    ga_keep = jnp.where(z_high == 1, ga[1], ga[0])
    ga_tile = ga_keep + swap(ga_send, "row", 4)

    m_pair = contract(zz[None], vertex, b_pair[None], a_wide)
    m_far = contract((zz ^ 2)[None], vertex, b_far[None], a_wide)

    gb_near = jnp.stack([dot_tn(b_pair, b_factor), dot_tn(b_far, b_factor)])
    gb_rest = jnp.stack([dot_tn(b_rest[0], b_factor), dot_tn(b_rest[1], b_factor)])
    odd = (core ^ (zz & 1)) == 1
    gb = jnp.where(odd, gb_rest, gb_near) + swap(jnp.where(odd, gb_near, gb_rest), "col", 1)
    odd = (y_bit ^ (zz >> 1)) == 1
    gb_tile = jnp.where(odd, gb[1], gb[0]) + swap(jnp.where(odd, gb[0], gb[1]), "col", 2)

    down = lax.broadcasted_iota(jnp.int32, (wide, narrow), 0) + col * wide
    across = lax.broadcasted_iota(jnp.int32, (wide, narrow), 1) + row * narrow
    tile = ga_tile.T * gb_tile + jnp.where(down == across, ridge_term, 0.0)

    pieces, tiles = [tile[None]], [[(0, 0)]]
    for axis, bit in (("row", 4), ("row", 2), ("row", 1), ("col", 2)):
        pieces.append(swap(jnp.concatenate(pieces) if len(pieces) > 1 else pieces[0], axis, bit))
        offset = (bit, 0) if axis == "row" else (0, bit)
        tiles.append([(r ^ offset[0], c ^ offset[1]) for piece in tiles for r, c in piece])
    pieces += [swap(piece, "col", 1) for piece in pieces]
    tiles += [[(r, c ^ 1) for r, c in piece] for piece in tiles]

    m_rest = contract(jnp.stack([zz ^ 1, zz ^ 3]), vertex, b_rest, a_wide)
    m_near = ordered(zz >= 2, m_pair, m_far, 0).reshape(2, fields, wide)
    m_rest = m_rest.reshape(fields, 2, wide).transpose(1, 0, 2)
    m_rest = jnp.where(zz >= 2, m_rest[::-1], m_rest)
    m_part = jnp.where(
        z_low == 1, jnp.stack([m_rest, m_near], axis=1), jnp.stack([m_near, m_rest], axis=1)
    )
    m_part = m_part.transpose(2, 0, 1, 3).reshape(2, fields // 2, rank)
    m_half = jnp.where(core == 1, m_part[1], m_part[0])
    m_half = m_half + swap(jnp.where(core == 1, m_part[0], m_part[1]), "col", 1)
    for axis, bit in (("col", 2), ("row", 1), ("row", 2), ("row", 4)):
        m_half = m_half + swap(m_half, axis, bit)
    m_total = ordered(core == 1, m_half, swap(m_half, "col", 1), 0)

    solved = solve(jnp.stack([row, col]), pieces, tiles, m_total)
    return lax.dynamic_slice_in_dim(solved, col * wide, wide, 1)


def general(vertex, a_factor, b_factor):
    fields, p_local, q_local = vertex.shape
    rank_cols, row_rank = a_factor.shape[1], b_factor.shape[1]
    a_rows = lax.all_gather(a_factor, "col", axis=1, tiled=True)
    b_rows = lax.all_gather(b_factor, "row", axis=1, tiled=True)
    rank = a_rows.shape[1]
    a_wide = a_rows.astype(jnp.float32)

    def one_field(slab):
        product = jnp.dot(slab, b_rows, preferred_element_type=jnp.float32)
        return jnp.sum(product * a_wide, axis=0)

    m_total = lax.psum(lax.map(one_field, vertex), ("row", "col"))
    ga_tile = lax.psum_scatter(dot_tn(a_factor, a_rows), "row", scatter_dimension=1, tiled=True)
    gb_tile = lax.psum_scatter(dot_tn(b_factor, b_rows), "col", scatter_dimension=1, tiled=True)
    tiles = lax.all_gather((ga_tile * gb_tile.T)[None], ("row", "col"), axis=0, tiled=True)
    weight = (
        tiles.reshape(lax.axis_size("row"), lax.axis_size("col"), rank_cols, row_rank)
        .transpose(1, 2, 0, 3)
        .reshape(rank, rank)
    )
    weight = weight + ridge_term * jnp.eye(rank, dtype=jnp.float32)
    columns = weight.reshape(rank, rank // NB, NB).transpose(1, 0, 2)
    pieces, tiles = [columns[k][None] for k in range(rank // NB)], [[(k, 0)] for k in range(rank // NB)]
    solved = solve(jnp.zeros((2,), jnp.int32), pieces, tiles, m_total)
    return lax.dynamic_slice_in_dim(solved, lax.axis_index("col") * rank_cols, rank_cols, 1)


def on_device(vertex, a_factor, b_factor):
    rows, cols = lax.axis_size("row"), lax.axis_size("col")
    aligned = a_factor.shape[1] == 2 * NB and b_factor.shape[1] == NB
    if rows == 8 and cols == 4 and aligned:
        return fast(vertex, a_factor, b_factor)
    return general(vertex, a_factor, b_factor)


def solution(mesh):
    return jax.shard_map(
        on_device,
        mesh=mesh,
        in_specs=(P(None, "row", "col"), P("row", "col"), P("col", "row")),
        out_specs=P(None, "col"),
        check_vma=False,
    )
```

time: 678 us -> 321 us (0.47)
  other arithmetic: 261 us -> 11.9 us
  Pallas kernels: 0 us -> 187 us
  matrix products: 132 us -> 7.16 us
  local copies, waits for them, and re-layouts: 101 us -> 6.8 us
  waiting for transfers between devices: 157 us -> 81.2 us
  starting transfers between devices: 0.2 us -> 25.7 us
  between operations: 19.6 us -> 0.44 us
    another operation x33 -> x5, other arithmetic: 252 us -> 1.33 us  [the longest x1 1.07 us: fast(): b_half = jnp.stack([b_pair, b_far])]
    pallas_call x0 -> x4, Pallas kernels: none -> 187 us  [the longest x3 101 us: contract(): pl.pallas_call(contract_kernel, out_shape=jax.ShapeDtypeStruct((fields //...]
    reduce_scatter x2 -> x0, waiting for transfers between devices: 85 us -> none  [the longest x1 61.8 us: on_device(): ga_tile = lax.psum_scatter(ga_part, 'row', scatter_dimension=1, tiled=True)]
    ppermute x0 -> x25, waiting for transfers between devices: none -> 81.2 us  [swap(): lax.ppermute(v, axis, [(s, s ^ bit) for s in range(lax.axis_size(axis))])]
    dot_general x18 -> x5, matrix products: 82.8 us -> 7.16 us  [dot_tn(): lax.dot_general(x, y, (((0,), (0,)), ((), ())), preferred_element_type=jn...]
    all_gather x3 -> x0, waiting for transfers between devices: 70.6 us -> none  [the longest x1 50.2 us: on_device(): column_block = lax.all_gather(b_factor, 'row', axis=1, tiled=True)]
    another operation x44 -> x0, matrix products: 48.8 us -> none  [the longest x14 26.2 us: on_device(): factor_lower = jnp.linalg.cholesky(weight)]
    dynamic_slice x17 -> x1, local copies, waits for them, and re-layouts: 45.4 us -> 0.64 us  [fast(): return lax.dynamic_slice_in_dim(solved, col * wide, wide, 1)]
  transfers between devices with their start and end apart: 6 -> 25, of which waited for: 4 -> 15; matrix products, arithmetic and copies ran while one was open for 69% -> 6% of each run, Pallas kernels for 0% -> 31%
where the time goes in v1:
time: 321 us; the launch traced here: 320 us
  Pallas kernels  187 us (58%)
  waiting for transfers between devices  81.2 us (25%)
  starting transfers between devices  25.7 us (8%)
  other arithmetic  11.9 us (4%)
  matrix products  7.16 us (2%)
  local copies, waits for them, and re-layouts  6.8 us (2%)
    pallas_call x3, Pallas kernels, contract(): pl.pallas_call(contract_kernel, out_shape=jax.ShapeDtypeStruct((fields //...  101 us
    pallas_call x1, Pallas kernels, solve(): pl.pallas_call(functools.partial(solve_kernel, tiles), out_shape=jax.Shap...  86.2 us
    ppermute x25, waiting for transfers between devices, swap(): lax.ppermute(v, axis, [(s, s ^ bit) for s in range(lax.axis_size(axis))])  81.2 us
    ppermute x25, starting transfers between devices, swap(): lax.ppermute(v, axis, [(s, s ^ bit) for s in range(lax.axis_size(axis))])  25.7 us
    dot_general x5, matrix products, dot_tn(): lax.dot_general(x, y, (((0,), (0,)), ((), ())), preferred_element_type=jn...  7.16 us
  transfers between devices with their start and end apart: 25, of which 15 were waited for; matrix products, arithmetic and copies ran while one was open for 6% of the time, Pallas kernels for 31%

profile of v1, /device:TPU:0, one launch (start us, length us, event | category | flops | bytes accessed | tf_op | source)
XLA Modules:
  0.0 320.3 jit_solution(14290095023529128119)
XLA Ops:
  0.0 3.0 collective-permute-start
  3.0 6.5 %collective-permute-done = bf16[512,256]{1,0:T(8,128)(2,1)S(1)} collective-permute-done((bf16[512,256]{1,0:T(8,128)(2,1)}, bf16[512,256]{1,0:T(8,128)(2,1)S(1)}, u32[]{:S(2)}, u32[]{:S(2)}) %collective-permute-start) | collective-permute-done | bytes 262176 | tf_op jit(solution)/shard_map/ppermute | solution.py:205
  9.5 1.2 maximum_select_fusion
  10.7 1.8 collective-permute-start.5
  12.5 7.2 %collective-permute-done.5 = bf16[1024,128]{1,0:T(8,128)(2,1)S(1)} collective-permute-done((bf16[1024,128]{1,0:T(8,128)(2,1)}, bf16[1024,128]{1,0:T(8,128)(2,1)S(1)}, u32[]{:S(2)}, u32[]{:S(2)}) %collective-permute-start.5) | collective-permute-done | bytes 262176 | tf_op jit(solution)/shard_map/ppermute | solution.py:205
  19.6 2.0 maximum_select_fusion.3
  21.6 2.8 collective-permute-start.6
  24.4 0.1 reshape.232
  24.6 1.2 broadcast_select_fusion.1
  25.9 1.1 copy.14
  27.0 0.8 reshape.233
  27.7 1.3 copy.26
  29.1 1.7 fusion.3
  30.9 1.6 collective-permute-start.2
  32.4 1.2 maximum_select_fusion.2.b_ref
  33.6 14.0 %collective-permute-done.6 = bf16[1024,256]{1,0:T(8,128)(2,1)S(1)} collective-permute-done((bf16[1024,256]{1,0:T(8,128)(2,1)}, bf16[1024,256]{1,0:T(8,128)(2,1)S(1)}, u32[]{:S(2)}, u32[]{:S(2)}) %collective-permute-start.6) | collective-permute-done | bytes 524320 | tf_op jit(solution)/shard_map/ppermute | solution.py:205
  47.6 1.1 pad_maximum_fusion.1
  48.7 0.8 collective-permute-start.7
  49.5 1.4 convolution_bitcast_fusion.1
  51.0 1.3 convolution_bitcast_fusion
  52.3 0.1 fusion.1
  52.4 0.1 copy.28
  52.6 0.1 copy.29
  52.7 1.3 collective-permute-start.3
  54.0 21.0 %collective-permute-done.7.b_ref = bf16[2,1024,256]{2,1,0:T(8,128)(2,1)S(1)} collective-permute-done((bf16[2,1024,256]{2,1,0:T(8,128)(2,1)}, bf16[2,1024,256]{2,1,0:T(8,128)(2,1)S(1)}, u32[]{:S(2)}, u32[]{:S(2)}) %collective-permute-start.7) | collective-permute-done | bytes 1048608 | tf_op jit(solution)/shard_map/ppermute | solution.py:205
  75.0 1.5 convolution_bitcast_fusion.2
  76.5 1.3 convolution_bitcast_fusion.3
  77.9 0.8 collective-permute-done.3
  78.8 3.3 %collective-permute-start.4 = (f32[128,256]{0,1:T(8,128)S(1)}, f32[128,256]{0,1:T(8,128)S(1)}, u32[]{:S(2)}, u32[]{:S(2)}) collective-permute-start(f32[128,256]{0,1:T(8,128)S(1)} %select_bitcast_fusion.3), channel_id=1, source_target_pairs={{0,16},{4,20},{8,24},{12,28},{16,0},{20,4},{24,8},{28,12},{1,17},{... | collective-permute-start | bytes 393224 | tf_op jit(solution)/shard_map/ppermute | solution.py:205
  82.2 1.6 collective-permute-start.9
  83.8 4.3 %collective-permute-done.4 = f32[128,256]{0,1:T(8,128)S(1)} collective-permute-done((f32[128,256]{0,1:T(8,128)S(1)}, f32[128,256]{0,1:T(8,128)S(1)}, u32[]{:S(2)}, u32[]{:S(2)}) %collective-permute-start.4) | collective-permute-done | bytes 131104 | tf_op jit(solution)/shard_map/ppermute | solution.py:205
  88.1 0.1 fusion.9.refs_0_
  88.4 1.5 convert_element_type.3.a_ref
  89.8 7.0 %collective-permute-done.10.refs_1_ = f32[1,256,128]{2,1,0:T(8,128)S(1)} collective-permute-done((f32[1,256,128]{2,1,0:T(8,128)S(1)}, f32[1,256,128]{2,1,0:T(8,128)S(1)}, u32[]{:S(2)}, u32[]{:S(2)}) %collective-permute-start.10) | collective-permute-done | bytes 131104 | tf_op jit(solution)/shard_map/ppermute | solution.py:205
  97.0 30.1 %shard_map.38 = f32[16,4,256]{2,1,0:T(4,128)S(1)} custom-call(s32[1]{0:T(128)} %bitcast.35.index, bf16[64,512,1024]{2,1,0:T(8,128)(2,1)} %v_ref.5, bf16[1,1024,256]{2,1,0:T(8,128)(2,1)S(1)} %bitcast.90, f32[512,1024]{1,0:T(8,128)S(1)} %convert_element_type.3.a_ref), custom_call_target="tpu_custom_call" | custom-call | flops 17179869184 | bytes 67108864 | tf_op jit(solution)/shard_map/pallas_call | solution.py:181
  127.1 0.7 copy-done
  127.8 0.9 pad_maximum_fusion.3
  128.6 1.5 collective-permute-start.12
  130.1 30.1 %shard_map.39 = f32[16,4,256]{2,1,0:T(4,128)S(1)} custom-call(s32[1]{0:T(128)} %bitcast.36.index, bf16[64,512,1024]{2,1,0:T(8,128)(2,1)} %v_ref.5, bf16[1,1024,256]{2,1,0:T(8,128)(2,1)S(1)} %maximum_select_fusion.2.b_ref, f32[512,1024]{1,0:T(8,128)S(1)} %convert_element_type.3.a_ref), custom_call_target="tpu_custom_call" | custom-call | flops 17179869184 | bytes 67108864 | tf_op jit(solution)/shard_map/pallas_call | solution.py:181
  160.3 2.1 pad_maximum_fusion.2
  162.4 1.5 collective-permute-start.13
  163.9 1.2 copy-done.3
  165.2 40.7 %shard_map.37 = f32[16,4,512]{2,1,0:T(4,128)S(1)} custom-call(s32[2]{0:T(128)S(1)} %pad_add_fusion.1.index, bf16[64,512,1024]{2,1,0:T(8,128)(2,1)} %v_ref.5, bf16[2,1024,256]{2,1,0:T(8,128)(2,1)S(1)} %copy-done.3, f32[512,1024]{1,0:T(8,128)S(1)} %convert_element_type.3.a_ref), custom_call_target="tpu_custom_call" | custom-call | flops 34359738368 | bytes 67108864 | tf_op jit(solution)/shard_map/pallas_call | solution.py:181
  205.9 0.1 reshape_reshape.3
  206.2 0.1 copy.24
  206.3 0.1 select_n.265
  206.4 0.6 collective-permute-start.19
  207.1 0.1 select_n.263
  207.2 1.8 collective-permute-done.19
  209.0 0.6 collective-permute-start.20
  209.6 5.0 %collective-permute-done.20 = f32[32,1024]{1,0:T(8,128)S(1)} collective-permute-done((f32[32,1024]{1,0:T(8,128)S(1)}, f32[32,1024]{1,0:T(8,128)S(1)}, u32[]{:S(2)}, u32[]{:S(2)}) %collective-permute-start.20) | collective-permute-done | bytes 131104 | tf_op jit(solution)/shard_map/ppermute | solution.py:205
  214.6 0.6 collective-permute-start.21
  215.2 4.4 %collective-permute-done.21 = f32[32,1024]{1,0:T(8,128)S(1)} collective-permute-done((f32[32,1024]{1,0:T(8,128)S(1)}, f32[32,1024]{1,0:T(8,128)S(1)}, u32[]{:S(2)}, u32[]{:S(2)}) %collective-permute-start.21) | collective-permute-done | bytes 131104 | tf_op jit(solution)/shard_map/ppermute | solution.py:205
  219.7 1.9 collective-permute-start.22
  221.6 3.1 collective-permute-done.22
  224.7 1.8 collective-permute-start.23
  226.5 4.1 %collective-permute-done.23 = f32[32,1024]{1,0:T(8,128)S(1)} collective-permute-done((f32[32,1024]{1,0:T(8,128)S(1)}, f32[32,1024]{1,0:T(8,128)S(1)}, u32[]{:S(2)}, u32[]{:S(2)}) %collective-permute-start.23) | collective-permute-done | bytes 131104 | tf_op jit(solution)/shard_map/ppermute | solution.py:205
  230.8 0.5 collective-permute-start.16
  231.3 0.8 collective-permute-done.24
  232.1 0.1 collective-permute-start.15
  232.3 0.3 collective-permute-done.14.refs_5_
  232.7 0.8 collective-permute-done.15.refs_6_
  233.5 86.2 %shard_map.40 = f32[64,1024]{1,0:T(8,128)S(1)} custom-call(s32[2]{0:T(128)S(1)} %pad_add_fusion.pos, f32[1,256,128]{2,1,0:T(8,128)S(1)} %fusion.9.refs_0_, f32[1,256,128]{2,1,0:T(8,128)S(1)} %collective-permute-done.10.refs_1_, f32[2,256,128]{2,1,0:T(8,128)S(1)} %copy-done.1, f32[4,256,128]{2,1,0:T(8,128)} %collective-permute-done.12.refs_3_, ...), custom_call_target="tpu_custom_call" | custom-call | flops 40000000000 | bytes 4194304 | tf_op jit(solution)/shard_map/pallas_call | solution.py:148
  319.6 0.6 constant_dynamic-slice_fusion
  (54 shorter events, 1.5 us)
Async XLA Ops:
  0.0 9.5 %collective-permute-start = (bf16[512,256]{1,0:T(8,128)(2,1)}, bf16[512,256]{1,0:T(8,128)(2,1)S(1)}, u32[]{:S(2)}, u32[]{:S(2)}) collective-permute-start(bf16[512,256]{1,0:T(8,128)(2,1)} %param.4), channel_id=1, source_target_pairs={{0,2},{1,3},{2,0},{3,1},{4,6},{5,7},{6,4},{7,5},{8,10},{9,11},{10,... | collective-permute-start | bytes 786440 | tf_op jit(solution)/shard_map/ppermute | solution.py:205
  10.6 13.8 %collective-permute-start.1 = (bf16[512,512]{1,0:T(8,128)(2,1)S(1)}, bf16[512,512]{1,0:T(8,128)(2,1)S(1)}, u32[]{:S(2)}, u32[]{:S(2)}) collective-permute-start(bf16[512,512]{1,0:T(8,128)(2,1)S(1)} %maximum_select_fusion), channel_id=1, source_target_pairs={{0,1},{1,0},{2,3},{3,2},{4,5},{5,4},{6,7},{7,6},{8,9},{9,8},{10,11... | collective-permute-start | bytes 1572872 | tf_op jit(solution)/shard_map/ppermute | solution.py:205
  10.7 8.9 %collective-permute-start.5 = (bf16[1024,128]{1,0:T(8,128)(2,1)}, bf16[1024,128]{1,0:T(8,128)(2,1)S(1)}, u32[]{:S(2)}, u32[]{:S(2)}) collective-permute-start(bf16[1024,128]{1,0:T(8,128)(2,1)} %param.5), channel_id=1, source_target_pairs={{0,4},{4,0},{8,12},{12,8},{16,20},{20,16},{24,28},{28,24},{1,5},{5... | collective-permute-start | bytes 786440 | tf_op jit(solution)/shard_map/ppermute | solution.py:205
  21.6 26.0 %collective-permute-start.6 = (bf16[1024,256]{1,0:T(8,128)(2,1)}, bf16[1024,256]{1,0:T(8,128)(2,1)S(1)}, u32[]{:S(2)}, u32[]{:S(2)}) collective-permute-start(bf16[1024,256]{1,0:T(8,128)(2,1)} %maximum_select_fusion.3), channel_id=1, source_target_pairs={{0,16},{4,20},{8,24},{12,28},{16,0},{20,4},{24,8},{28,12},{1,17},{... | collective-permute-start | bytes 1572872 | tf_op jit(solution)/shard_map/ppermute | solution.py:205
  27.7 19.9 %copy-start.4 = (bf16[512,1024]{1,0:T(8,128)(2,1)}, bf16[512,1024]{1,0:T(8,128)(2,1)S(1)}, u32[]{:S(2)}) copy-start(bf16[512,1024]{1,0:T(8,128)(2,1)S(1)} %reshape.233) | copy-start | bytes 3145732
  30.9 21.4 %collective-permute-start.2 = (f32[4,128,256]{2,1,0:T(8,128)S(1)}, f32[4,128,256]{2,1,0:T(8,128)S(1)}, u32[]{:S(2)}, u32[]{:S(2)}) collective-permute-start(f32[4,128,256]{2,1,0:T(8,128)S(1)} %select_bitcast_fusion), channel_id=1, source_target_pairs={{0,4},{4,0},{8,12},{12,8},{16,20},{20,16},{24,28},{28,24},{1,5},{5... | collective-permute-start | bytes 1572872 | tf_op jit(solution)/shard_map/ppermute | solution.py:205
  48.7 26.3 %collective-permute-start.7 = (bf16[2,1024,256]{2,1,0:T(8,128)(2,1)}, bf16[2,1024,256]{2,1,0:T(8,128)(2,1)S(1)}, u32[]{:S(2)}, u32[]{:S(2)}) collective-permute-start(bf16[2,1024,256]{2,1,0:T(8,128)(2,1)} %pad_maximum_fusion.1), channel_id=1, source_target_pairs={{0,8},{4,12},{8,0},{12,4},{16,24},{20,28},{24,16},{28,20},{1,9},{5... | collective-permute-start | bytes 3145736 | tf_op jit(solution)/shard_map/ppermute | solution.py:205
  52.7 26.0 %collective-permute-start.3 = (f32[2,128,256]{1,2,0:T(8,128)S(1)}, f32[2,128,256]{1,2,0:T(8,128)S(1)}, u32[]{:S(2)}, u32[]{:S(2)}) collective-permute-start(f32[2,128,256]{1,2,0:T(8,128)S(1)} %select_bitcast_fusion.1), channel_id=1, source_target_pairs={{0,8},{4,12},{8,0},{12,4},{16,24},{20,28},{24,16},{28,20},{1,9},{5... | collective-permute-start | bytes 786440 | tf_op jit(solution)/shard_map/ppermute | solution.py:205
  75.0 13.3 %copy-start.2 = (bf16[2,1024,256]{2,1,0:T(8,128)(2,1)}, bf16[2,1024,256]{2,1,0:T(8,128)(2,1)S(1)}, u32[]{:S(2)}) copy-start(bf16[2,1024,256]{2,1,0:T(8,128)(2,1)S(1)} %collective-permute-done.7.b_ref) | copy-start | bytes 3145732
  77.8 4.3 %collective-permute-start.8 = (f32[2,256,128]{2,1,0:T(8,128)S(1)}, f32[2,256,128]{2,1,0:T(8,128)S(1)}, u32[]{:S(2)}, u32[]{:S(2)}) collective-permute-start(f32[2,256,128]{2,1,0:T(8,128)S(1)} %fusion.5), channel_id=1, source_target_pairs={{0,1},{1,0},{2,3},{3,2},{4,5},{5,4},{6,7},{7,6},{8,9},{9,8},{10,11... | collective-permute-start | bytes 786440 | tf_op jit(solution)/shard_map/ppermute | solution.py:205
  78.8 9.3 %collective-permute-start.4 = (f32[128,256]{0,1:T(8,128)S(1)}, f32[128,256]{0,1:T(8,128)S(1)}, u32[]{:S(2)}, u32[]{:S(2)}) collective-permute-start(f32[128,256]{0,1:T(8,128)S(1)} %select_bitcast_fusion.3), channel_id=1, source_target_pairs={{0,16},{4,20},{8,24},{12,28},{16,0},{20,4},{24,8},{28,12},{1,17},{... | collective-permute-start | bytes 393224 | tf_op jit(solution)/shard_map/ppermute | solution.py:205
  82.2 5.9 %collective-permute-start.9 = (f32[256,128]{1,0:T(8,128)S(1)}, f32[256,128]{1,0:T(8,128)S(1)}, u32[]{:S(2)}, u32[]{:S(2)}) collective-permute-start(f32[256,128]{1,0:T(8,128)S(1)} %select_bitcast_fusion.2), channel_id=1, source_target_pairs={{0,2},{1,3},{2,0},{3,1},{4,6},{5,7},{6,4},{7,5},{8,10},{9,11},{10,... | collective-permute-start | bytes 393224 | tf_op jit(solution)/shard_map/ppermute | solution.py:205
  88.2 8.7 %collective-permute-start.10 = (f32[1,256,128]{2,1,0:T(8,128)S(1)}, f32[1,256,128]{2,1,0:T(8,128)S(1)}, u32[]{:S(2)}, u32[]{:S(2)}) collective-permute-start(f32[1,256,128]{2,1,0:T(8,128)S(1)} %fusion.9.refs_0_), channel_id=1, source_target_pairs={{0,16},{4,20},{8,24},{12,28},{16,0},{20,4},{24,8},{28,12},{1,17},{... | collective-permute-start | bytes 393224 | tf_op jit(solution)/shard_map/ppermute | solution.py:205
  96.9 30.2 %collective-permute-start.11 = (f32[2,256,128]{2,1,0:T(8,128)S(1)}, f32[2,256,128]{2,1,0:T(8,128)S(1)}, u32[]{:S(2)}, u32[]{:S(2)}) collective-permute-start(f32[2,256,128]{2,1,0:T(8,128)S(1)} %pad_maximum_fusion.6), channel_id=1, source_target_pairs={{0,8},{4,12},{8,0},{12,4},{16,24},{20,28},{24,16},{28,20},{1,9},{5... | collective-permute-start | bytes 786440 | tf_op jit(solution)/shard_map/ppermute | solution.py:205
  127.0 0.7 copy-start
  128.6 31.7 %copy-start.1 = (f32[2,256,128]{2,1,0:T(8,128)S(1)}, f32[2,256,128]{2,1,0:T(8,128)}, u32[]{:S(2)}) copy-start(f32[2,256,128]{2,1,0:T(8,128)} %copy-done) | copy-start | bytes 786436
  128.6 31.6 %collective-permute-start.12 = (f32[4,256,128]{2,1,0:T(8,128)}, f32[4,256,128]{2,1,0:T(8,128)}, u32[]{:S(2)}, u32[]{:S(2)}) collective-permute-start(f32[4,256,128]{2,1,0:T(8,128)} %pad_maximum_fusion.3), channel_id=1, source_target_pairs={{0,4},{4,0},{8,12},{12,8},{16,20},{20,16},{24,28},{28,24},{1,5},{5... | collective-permute-start | bytes 1572872 | tf_op jit(solution)/shard_map/ppermute | solution.py:205
  162.4 43.6 %collective-permute-start.13 = (f32[8,256,128]{2,1,0:T(8,128)}, f32[8,256,128]{2,1,0:T(8,128)}, u32[]{:S(2)}, u32[]{:S(2)}) collective-permute-start(f32[8,256,128]{2,1,0:T(8,128)} %pad_maximum_fusion.2), channel_id=1, source_target_pairs={{0,2},{1,3},{2,0},{3,1},{4,6},{5,7},{6,4},{7,5},{8,10},{9,11},{10,... | collective-permute-start | bytes 3145736 | tf_op jit(solution)/shard_map/ppermute | solution.py:205
  163.9 1.2 copy-start.3
  206.1 27.4 %collective-permute-start.18 = (f32[8,256,128]{2,1,0:T(8,128)}, f32[8,256,128]{2,1,0:T(8,128)S(1)}, u32[]{:S(2)}, u32[]{:S(2)}) collective-permute-start(f32[8,256,128]{2,1,0:T(8,128)} %collective-permute-done.13.refs_4_), channel_id=1, source_target_pairs={{0,1},{1,0},{2,3},{3,2},{4,5},{5,4},{6,7},{7,6},{8,9},{9,8},{10,11... | collective-permute-start | bytes 3145736 | tf_op jit(solution)/shard_map/ppermute | solution.py:205
  206.4 2.6 collective-permute-start.19
  209.0 5.6 %collective-permute-start.20 = (f32[32,1024]{1,0:T(8,128)S(1)}, f32[32,1024]{1,0:T(8,128)S(1)}, u32[]{:S(2)}, u32[]{:S(2)}) collective-permute-start(f32[32,1024]{1,0:T(8,128)S(1)} %add.60), channel_id=1, source_target_pairs={{0,2},{1,3},{2,0},{3,1},{4,6},{5,7},{6,4},{7,5},{8,10},{9,11},{10,... | collective-permute-start | bytes 393224 | tf_op jit(solution)/shard_map/ppermute | solution.py:205
  214.6 5.0 %collective-permute-start.21 = (f32[32,1024]{1,0:T(8,128)S(1)}, f32[32,1024]{1,0:T(8,128)S(1)}, u32[]{:S(2)}, u32[]{:S(2)}) collective-permute-start(f32[32,1024]{1,0:T(8,128)S(1)} %add.61), channel_id=1, source_target_pairs={{0,4},{4,0},{8,12},{12,8},{16,20},{20,16},{24,28},{28,24},{1,5},{5... | collective-permute-start | bytes 393224 | tf_op jit(solution)/shard_map/ppermute | solution.py:205
  219.7 5.0 %collective-permute-start.22 = (f32[32,1024]{1,0:T(8,128)S(1)}, f32[32,1024]{1,0:T(8,128)S(1)}, u32[]{:S(2)}, u32[]{:S(2)}) collective-permute-start(f32[32,1024]{1,0:T(8,128)S(1)} %add.62), channel_id=1, source_target_pairs={{0,8},{4,12},{8,0},{12,4},{16,24},{20,28},{24,16},{28,20},{1,9},{5... | collective-permute-start | bytes 393224 | tf_op jit(solution)/shard_map/ppermute | solution.py:205
  221.6 11.9 %collective-permute-start.17 = (f32[4,256,128]{2,1,0:T(8,128)}, f32[4,256,128]{2,1,0:T(8,128)S(1)}, u32[]{:S(2)}, u32[]{:S(2)}) collective-permute-start(f32[4,256,128]{2,1,0:T(8,128)} %collective-permute-done.12.refs_3_), channel_id=1, source_target_pairs={{0,1},{1,0},{2,3},{3,2},{4,5},{5,4},{6,7},{7,6},{8,9},{9,8},{10,11... | collective-permute-start | bytes 1572872 | tf_op jit(solution)/shard_map/ppermute | solution.py:205
  224.7 5.9 %collective-permute-start.23 = (f32[32,1024]{1,0:T(8,128)S(1)}, f32[32,1024]{1,0:T(8,128)S(1)}, u32[]{:S(2)}, u32[]{:S(2)}) collective-permute-start(f32[32,1024]{1,0:T(8,128)S(1)} %add.63), channel_id=1, source_target_pairs={{0,16},{4,20},{8,24},{12,28},{16,0},{20,4},{24,8},{28,12},{1,17},{... | collective-permute-start | bytes 393224 | tf_op jit(solution)/shard_map/ppermute | solution.py:205
  230.7 1.4 collective-permute-start.24
  230.8 2.7 collective-permute-start.16
  231.3 1.4 collective-permute-start.14
  232.1 1.3 collective-permute-start.15
